TPU v7x, 128 devices: a whole 4x4x4 slice. The times are simulated.
128 devices in a mesh: tile: 8 (over z_lo, x), blk: 16 (over y, z_hi, core).
Axes of the slice: x: 4, y: 4, z: 4 (z_hi: 2, z_lo: 2; z = z_hi * 2 + z_lo), core: 2. Of those that a mesh axis runs over, the one named last changes fastest.
Arguments:
- tiles: bfloat16 [6144, 8, 8, 2048], P(('blk', 'tile')), may hold values from -10 to 10
- w_reduce: bfloat16 [2048, 512], replicated, may hold values from -0.125 to 0.125
- w_spatial: bfloat16 [9, 512, 512], replicated, may hold values from -0.09375 to 0.09375
- w_expand: bfloat16 [512, 2048], replicated, may hold values from -0.25 to 0.25
- w_embed: bfloat16 [2048, 1536], replicated, may hold values from -0.125 to 0.125
- w_query: bfloat16 [1536, 1536], P(None, 'tile'), may hold values from -8 to 8
- w_key: bfloat16 [1536, 1536], P(None, 'tile'), may hold values from -200 to 200
- w_value: bfloat16 [1536, 1536], P(None, 'tile'), may hold values from -0.15625 to 0.15625
- w_out: bfloat16 [1536, 1536], P('tile'), may hold values from -0.15625 to 0.15625
- slide_tiles: int32 [4], replicated, may hold values from 1 to 4608, 6144 in all
Outputs:
- mixed: bfloat16 [6144, 1536], P(('blk', 'tile'))
Inputs may be any that keep to these rules, and one draw needn't show every extreme that they name: `slide_tiles`: the counts sum to 6144 and the largest is exactly 4608.
All inputs are finite; a program needn't handle non-finite values.
Results may differ from a plain program's by a relative error of at most 0.017.
Values may be sent and summed in bfloat16 or wider, within the bound.
A program may use at most 256 MiB of HBM per device.

v0:
```python
import math
import jax
import jax.numpy as jnp
from jax import lax
from jax.sharding import PartitionSpec as P

C = 2048
MID = 512
SIDE = 8
HD = 96


def encode(block, w_reduce, w_spatial, w_expand, w_embed):
    count = block.shape[0]
    flat = block.reshape(count * SIDE * SIDE, C)
    reduced = jax.nn.relu(jnp.dot(flat, w_reduce, preferred_element_type=jnp.float32)).astype(
        jnp.bfloat16
    )
    reduced = reduced.reshape(count, SIDE, SIDE, MID)
    padded = jnp.pad(reduced, ((0, 0), (1, 1), (1, 1), (0, 0)))
    summed = jnp.zeros((count * SIDE * SIDE, MID), jnp.float32)
    for tap in range(9):
        row_off = tap // 3
        col_off = tap % 3
        window = padded[:, row_off : row_off + SIDE, col_off : col_off + SIDE, :].reshape(
            count * SIDE * SIDE, MID
        )
        summed = summed + jnp.dot(window, w_spatial[tap], preferred_element_type=jnp.float32)
    spatial = jax.nn.relu(summed).astype(jnp.bfloat16)
    output = jax.nn.relu(
        flat.astype(jnp.float32) + jnp.dot(spatial, w_expand, preferred_element_type=jnp.float32)
    )
    pooled = (jnp.sum(output.reshape(count, SIDE * SIDE, C), axis=1) / (SIDE * SIDE)).astype(
        jnp.bfloat16
    )
    return jnp.dot(pooled, w_embed, preferred_element_type=jnp.float32).astype(jnp.bfloat16)


def normalize(rows):
    values = rows.astype(jnp.float32)
    center = jnp.mean(values, axis=1, keepdims=True)
    spread = jnp.mean((values - center) ** 2, axis=1, keepdims=True)
    return ((values - center) * lax.rsqrt(spread + 1e-05)).astype(jnp.bfloat16)


def slide_of(positions, slide_tiles):
    ends = jnp.cumsum(slide_tiles)[:-1]
    return jnp.sum((positions[:, None] >= ends[None, :]).astype(jnp.int32), axis=1)


def shards(
    tiles, w_reduce, w_spatial, w_expand, w_embed, w_query, w_key, w_value, w_out, slide_tiles
):
    emb = encode(tiles, w_reduce, w_spatial, w_expand, w_embed)
    width = w_query.shape[1]
    heads_here = width // HD
    w_joined = jnp.concatenate([w_query, w_key, w_value], axis=1)
    joined = jnp.dot(
        normalize(lax.all_gather(emb, "tile", axis=0, tiled=True)),
        w_joined,
        preferred_element_type=jnp.float32,
    ).astype(jnp.bfloat16)
    length = joined.shape[0]
    query = joined[:, :width].reshape(length, heads_here, HD)
    key_value = joined[:, width:]
    query_pos = lax.axis_index("blk") * length + jnp.arange(length, dtype=jnp.int32)
    query_slide = slide_of(query_pos, slide_tiles)
    scale = 1.0 / math.sqrt(HD)
    piece = lax.all_gather(key_value, "blk", axis=0, tiled=True)
    rows = piece.shape[0]
    key_pos = jnp.arange(rows, dtype=jnp.int32)
    same = query_slide[:, None] == slide_of(key_pos, slide_tiles)[None, :]
    top_old = jnp.full((heads_here, length), -1e30, jnp.float32)
    keys = piece[:, :width].reshape(rows, heads_here, HD)
    values = piece[:, width:].reshape(rows, heads_here, HD)
    scores = jnp.einsum("qhd,khd->hqk", query, keys, preferred_element_type=jnp.float32) * scale
    scores = jnp.where(same[None], scores, -1e30)
    top_new = jnp.maximum(top_old, jnp.max(scores, axis=2))
    probs = jnp.where(same[None], jnp.exp(scores - top_new[:, :, None]), 0.0)
    total_new = jnp.sum(probs, axis=2)
    accum_new = jnp.einsum(
        "hqk,khd->hqd", probs.astype(jnp.bfloat16), values, preferred_element_type=jnp.float32
    )
    attended = (
        (accum_new / total_new[:, :, None])
        .transpose(1, 0, 2)
        .reshape(length, width)
        .astype(jnp.bfloat16)
    )
    summed = lax.psum_scatter(
        jnp.dot(attended, w_out, preferred_element_type=jnp.float32).astype(jnp.bfloat16),
        "tile",
        scatter_dimension=0,
        tiled=True,
    ).astype(jnp.float32)
    return (emb.astype(jnp.float32) + summed).astype(jnp.bfloat16)


def solution(mesh):
    placed = (
        P(("blk", "tile"), None, None, None),
        P(),
        P(),
        P(),
        P(),
        P(None, "tile"),
        P(None, "tile"),
        P(None, "tile"),
        P("tile", None),
        P(),
    )
    return jax.shard_map(
        shards, mesh=mesh, in_specs=placed, out_specs=P(("blk", "tile"), None), check_vma=False
    )
```

profile of v0, /device:TPU:0, one launch (start us, length us, event | category | flops | bytes accessed | tf_op | source)
XLA Modules:
  0.0 305.9 jit_solution(4576410972492332639)
XLA Ops:
  6.5 13.1 %maximum_convert_fusion.1 = bf16[3072,512]{1,0:T(8,128)(2,1)} fusion(bf16[3072,2048]{1,0:T(8,128)(2,1)} %bitcast.73, bf16[2048,512]{1,0:T(8,128)(2,1)} %param.11), kind=kOutput, calls=%fused_computation.17 | convolution fusion | flops 6445596672 | bytes 17825792 | tf_op jit(solution)/shard_map/dot_general | solution.py:16
  19.6 13.5 %pad_slice_fusion = (bf16[48,8,8,512]{3,2,1,0:T(8,128)(2,1)}, bf16[48,8,8,512]{3,2,1,0:T(8,128)(2,1)S(1)}, bf16[48,8,8,512]{3,2,1,0:T(8,128)(2,1)S(1)}, bf16[48,...) fusion(bf16[48,8,8,512]{3,2,1,0:T(8,128)(2,1)} %bitcast.83), kind=kLoop, calls=%fused_computation.3 | loop fusion | bytes 28311552 | tf_op jit(solution)/shard_map/slice | solution.py:25
  33.2 6.6 %fusion.40 = f32[3072,512]{1,0:T(8,128)} fusion(bf16[3072,512]{1,0:T(8,128)(2,1)} %maximum_convert_fusion.1, bf16[9,512,512]{2,1,0:T(8,128)(2,1)} %param.12), kind=kOutput, calls=%fused_computation.46 | convolution fusion | flops 1610612736 | bytes 9961472 | tf_op jit(solution)/shard_map/dot_general | solution.py:28
  39.8 4.5 %fusion.34 = f32[3072,512]{1,0:T(8,128)} fusion(bf16[3072,512]{1,0:T(8,128)(2,1)S(1)} %bitcast.82, bf16[9,512,512]{2,1,0:T(8,128)(2,1)S(1)} %copy-done.4), kind=kOutput, calls=%fused_computation.40 | convolution fusion | flops 1610612736 | bytes 9961472 | tf_op jit(solution)/shard_map/dot_general | solution.py:28
  44.3 4.5 %fusion.36 = f32[3072,512]{1,0:T(8,128)} fusion(bf16[3072,512]{1,0:T(8,128)(2,1)S(1)} %bitcast.81, bf16[9,512,512]{2,1,0:T(8,128)(2,1)S(1)} %copy-done.4), kind=kOutput, calls=%fused_computation.42 | convolution fusion | flops 1610612736 | bytes 9961472 | tf_op jit(solution)/shard_map/dot_general | solution.py:28
  48.8 4.4 %fusion.38 = f32[3072,512]{1,0:T(8,128)} fusion(bf16[3072,512]{1,0:T(8,128)(2,1)S(1)} %bitcast.80, bf16[9,512,512]{2,1,0:T(8,128)(2,1)S(1)} %copy-done.4), kind=kOutput, calls=%fused_computation.44 | convolution fusion | flops 1610612736 | bytes 9961472 | tf_op jit(solution)/shard_map/dot_general | solution.py:28
  53.2 4.4 %fusion.42 = f32[3072,512]{1,0:T(8,128)} fusion(bf16[3072,512]{1,0:T(8,128)(2,1)S(1)} %bitcast.79, bf16[9,512,512]{2,1,0:T(8,128)(2,1)S(1)} %copy-done.4), kind=kOutput, calls=%fused_computation.48 | convolution fusion | flops 1610612736 | bytes 9961472 | tf_op jit(solution)/shard_map/dot_general | solution.py:28
  57.7 4.5 %fusion.44 = f32[3072,512]{1,0:T(8,128)} fusion(bf16[3072,512]{1,0:T(8,128)(2,1)S(1)} %bitcast.78, bf16[9,512,512]{2,1,0:T(8,128)(2,1)S(1)} %copy-done.4), kind=kOutput, calls=%fused_computation.50 | convolution fusion | flops 1610612736 | bytes 9961472 | tf_op jit(solution)/shard_map/dot_general | solution.py:28
  62.1 4.4 %fusion.46 = f32[3072,512]{1,0:T(8,128)} fusion(bf16[3072,512]{1,0:T(8,128)(2,1)S(1)} %bitcast.77, bf16[9,512,512]{2,1,0:T(8,128)(2,1)S(1)} %copy-done.4), kind=kOutput, calls=%fused_computation.52 | convolution fusion | flops 1610612736 | bytes 9961472 | tf_op jit(solution)/shard_map/dot_general | solution.py:28
  66.6 4.5 %fusion.48 = f32[3072,512]{1,0:T(8,128)} fusion(bf16[3072,512]{1,0:T(8,128)(2,1)S(1)} %bitcast.76, bf16[9,512,512]{2,1,0:T(8,128)(2,1)S(1)} %copy-done.4), kind=kOutput, calls=%fused_computation.54 | convolution fusion | flops 1610612736 | bytes 9961472 | tf_op jit(solution)/shard_map/dot_general | solution.py:28
  71.0 33.0 %add_maximum_fusion = f32[3072,2048]{1,0:T(8,128)} fusion(bf16[3072,2048]{1,0:T(8,128)(2,1)} %bitcast.74, bf16[512,2048]{1,0:T(8,128)(2,1)S(1)} %copy-done, f32[3072,512]{1,0:T(8,128)} %fusion.34, f32[3072,512]{1,0:T(8,128)} %fusion.36, f32[3072,512]{1,0:T(8,128)} %fusion.38, f32[3072,512]{1,0:T(8,128)} %fusion.40, f32[3072,512]{1,0:T(8,128)} %fusion.42, ...), kind=kOutput, calls=%fused_computation | convolution fusion | flops 8087666688 | bytes 93847552 | tf_op jit(solution)/shard_map/dot_general | solution.py:31
  104.0 9.5 %reduce_sum.54 = f32[48,2048]{1,0:T(8,128)S(1)} reduce(f32[48,64,2048]{2,1,0:T(8,128)} %bitcast.72, f32[]{:T(128)} %constant.11.clone.1), dimensions={1}, to_apply=%region_0.1 | reduce | flops 6193152 | bytes 25559044 | tf_op jit(solution)/shard_map/reduce_sum | solution.py:33
  113.6 4.7 %convolution_convert_fusion.1 = bf16[48,1536]{1,0:T(8,128)(2,1)} fusion(bf16[2048,1536]{1,0:T(8,128)(2,1)} %param.14, f32[48,2048]{1,0:T(8,128)S(1)} %reduce_sum.54), kind=kOutput, calls=%fused_computation.26 | convolution fusion | flops 302260224 | bytes 6832128 | tf_op jit(solution)/shard_map/dot_general | solution.py:36
  118.4 41.8 %all-gather.3.cloned.1.call-done = bf16[384,1536]{1,0:T(8,128)(2,1)} async-done(((bf16[48,1536]{1,0:T(8,128)(2,1)}), bf16[384,1536]{1,0:T(8,128)(2,1)}) %all-gather.3.cloned.1.call-update) | async-done | bytes 1179664 | tf_op jit(solution)/shard_map/all_gather | solution.py:59
  161.7 1.7 fusion.8
  163.5 2.5 fusion.16
  167.2 2.9 broadcast_compare_fusion
  170.1 57.6 %all-gather.5.cloned.1.call-done = bf16[6144,384]{0,1:T(8,128)(2,1)} async-done(((bf16[384,384]{0,1:T(8,128)(2,1)}), bf16[6144,384]{0,1:T(8,128)(2,1)}) %all-gather.5.cloned.1.call-update) | async-done | bytes 4718608 | tf_op jit(solution)/shard_map/all_gather | solution.py:69
  227.7 5.1 %fusion.67 = (bf16[6144,192]{0,1:T(8,128)(2,1)}, bf16[6144,192]{0,1:T(8,128)(2,1)}) fusion(bf16[6144,384]{0,1:T(8,128)(2,1)} %all-gather.5.cloned.1.call-done), kind=kLoop, calls=%fused_computation.82 | loop fusion | bytes 9437184 | tf_op jit(solution)/shard_map/slice | solution.py:74
  232.8 6.4 %fusion = (f32[2,384]{1,0:T(2,128)S(1)}, f32[2,384,6144]{2,1,0:T(8,128)S(1)}) fusion(pred[384,6144]{1,0:T(8,128)(4,1)} %broadcast_compare_fusion, bf16[384,2,96]{0,2,1:T(8,128)(2,1)S(1)} %bitcast.86, bf16[6144,2,96]{0,2,1:T(8,128)(2,1)} %bitcast.85), kind=kOutput, calls=%fused_computation.11 | convolution fusion | flops 920124672 | bytes 23743488 | tf_op jit(solution)/shard_map/qhd,khd->hqk/dot_general | solution.py:76
  239.2 8.0 %fusion.1 = f32[2,384]{1,0:T(2,128)S(1)} fusion(f32[2,384,6144]{2,1,0:T(8,128)S(1)} %get-tuple-element.16, f32[2,384]{1,0:T(2,128)S(1)} %broadcast_maximum_fusion, pred[384,6144]{1,0:T(8,128)(4,1)} %broadcast_compare_fusion), kind=kLoop, calls=%fused_computation.12 | loop fusion | flops 23592192 | bytes 21239808 | tf_op jit(solution)/shard_map/reduce_sum | solution.py:80
  247.2 10.9 %fusion.28 = bf16[384,2,96]{0,2,1:T(8,128)(2,1)S(1)} fusion(bf16[6144,2,96]{0,2,1:T(8,128)(2,1)} %bitcast.84, f32[2,384,6144]{2,1,0:T(8,128)} %copy-done.2, f32[2,384]{1,0:T(2,128)S(1)} %broadcast_maximum_fusion, pred[384,6144]{1,0:T(8,128)(4,1)} %broadcast_compare_fusion, f32[384,2]{0,1:T(2,128)S(1)} %bitcast.88), kind=kOutput, calls=%fused_computation.38 | convolution fusion | flops 929710080 | bytes 23746560 | tf_op jit(solution)/shard_map/hqk,khd->hqd/dot_general | solution.py:81
  259.7 38.1 %reduce-scatter.2.cloned.1.call-done = bf16[48,1536]{1,0:T(8,128)(2,1)} async-done(((bf16[384,1536]{1,0:T(8,128)(2,1)}), bf16[48,1536]{1,0:T(8,128)(2,1)}) %reduce-scatter.2.cloned.1.call-update) | async-done | bytes 147472 | tf_op jit(solution)/shard_map/reduce_scatter | solution.py:90
  297.8 1.6 add_convert_fusion
  (40 shorter events, 4.4 us)
Async XLA Ops:
  6.5 64.5 %copy-start = (bf16[512,2048]{1,0:T(8,128)(2,1)S(1)}, bf16[512,2048]{1,0:T(8,128)(2,1)}, u32[]{:S(2)}) copy-start(bf16[512,2048]{1,0:T(8,128)(2,1)} %param.13) | copy-start | bytes 6291460
  6.5 153.6 %all-gather.3.cloned.1.call-start = ((), (), s32[]{:S(2)}) async-start(), calls=%async_computation.1 | async-start | bytes 1327104 | tf_op jit(solution)/shard_map/all_gather | solution.py:59
  33.1 6.7 %copy-start.3 = (bf16[48,8,8,512]{3,2,1,0:T(8,128)(2,1)S(1)}, bf16[48,8,8,512]{3,2,1,0:T(8,128)(2,1)}, u32[]{:S(2)}) copy-start(bf16[48,8,8,512]{3,2,1,0:T(8,128)(2,1)} %get-tuple-element.13) | copy-start | bytes 9437188
  33.1 6.7 %copy-start.4 = (bf16[9,512,512]{2,1,0:T(8,128)(2,1)S(1)}, bf16[9,512,512]{2,1,0:T(8,128)(2,1)}, u32[]{:S(2)}) copy-start(bf16[9,512,512]{2,1,0:T(8,128)(2,1)} %param.12) | copy-start | bytes 14155780
  113.6 49.9 %copy-start.7 = (bf16[1536,192]{0,1:T(8,128)(2,1)S(1)}, bf16[1536,192]{0,1:T(8,128)(2,1)}, u32[]{:S(2)}) copy-start(bf16[1536,192]{0,1:T(8,128)(2,1)} %param.17) | copy-start | bytes 1769476
  113.6 49.8 %copy-start.8 = (bf16[1536,192]{0,1:T(8,128)(2,1)S(1)}, bf16[1536,192]{0,1:T(8,128)(2,1)}, u32[]{:S(2)}) copy-start(bf16[1536,192]{0,1:T(8,128)(2,1)} %param.16) | copy-start | bytes 1769476
  113.6 49.8 %copy-start.9 = (bf16[1536,192]{0,1:T(8,128)(2,1)S(1)}, bf16[1536,192]{0,1:T(8,128)(2,1)}, u32[]{:S(2)}) copy-start(bf16[1536,192]{0,1:T(8,128)(2,1)} %param.15) | copy-start | bytes 1769476
  118.3 109.3 %all-gather.5.cloned.1.call-start = ((), (), s32[]{:S(2)}) async-start(), calls=%async_computation.2 | async-start | bytes 5013504 | tf_op jit(solution)/shard_map/all_gather | solution.py:69
  163.4 3.3 %copy-start.10 = (s32[4]{0:T(128)S(1)}, s32[4]{0:T(128)}, u32[]{:S(2)}) copy-start(s32[4]{0:T(128)} %param.19) | copy-start | bytes 52
  166.7 131.1 %reduce-scatter.2.cloned.1.call-start = ((), (), s32[]{:S(2)}) async-start(), calls=%async_computation.3 | async-start | bytes 1327104 | tf_op jit(solution)/shard_map/reduce_scatter | solution.py:90
  239.2 8.0 %copy-start.2 = (f32[2,384,6144]{2,1,0:T(8,128)}, f32[2,384,6144]{2,1,0:T(8,128)S(1)}, u32[]{:S(2)}) copy-start(f32[2,384,6144]{2,1,0:T(8,128)S(1)} %get-tuple-element.16) | copy-start | bytes 56623108
  247.2 10.9 %copy-start.6 = (bf16[192,1536]{1,0:T(8,128)(2,1)S(1)}, bf16[192,1536]{1,0:T(8,128)(2,1)}, u32[]{:S(2)}) copy-start(bf16[192,1536]{1,0:T(8,128)(2,1)} %param.18) | copy-start | bytes 1769476
  247.2 50.6 %copy-start.5 = (bf16[48,1536]{1,0:T(8,128)(2,1)S(1)}, bf16[48,1536]{1,0:T(8,128)(2,1)}, u32[]{:S(2)}) copy-start(bf16[48,1536]{1,0:T(8,128)(2,1)} %convolution_convert_fusion.1) | copy-start | bytes 442372
  247.2 52.2 %copy-start.1 = (bf16[512,2048]{1,0:T(8,128)(2,1)S(1)}, bf16[512,2048]{1,0:T(8,128)(2,1)}, u32[]{:S(2)}) copy-start(bf16[512,2048]{1,0:T(8,128)(2,1)} %param.13) | copy-start | bytes 6291460
Sparse Core Ops, SparseCore 0:
  118.4 41.6 all-gather.2
  166.8 60.7 all-gather.4
  259.8 37.9 reduce-scatter.1
where the time goes:
time: 306 us
  waiting for transfers between devices  138 us (45%)
  matrix products  110 us (36%)
  other arithmetic  25.6 us (8%)
  local copies, waits for them, and re-layouts  19.4 us (6%)
  between operations  13.3 us (4%)
    all_gather x1, waiting for transfers between devices, shards(): piece = lax.all_gather(key_value, 'blk', axis=0, tiled=True)  57.6 us
    all_gather x1, waiting for transfers between devices, shards(): lax.all_gather(emb, 'tile', axis=0, tiled=True)  41.8 us
    reduce_scatter x1, waiting for transfers between devices, shards(): lax.psum_scatter(jnp.dot(attended, w_out, preferred_element_type=jnp.floa...  38.1 us
    dot_general x8, matrix products, encode(): jnp.dot(window, w_spatial[tap], preferred_element_type=jnp.float32)  37.9 us
    dot_general x1, matrix products, encode(): jnp.dot(spatial, w_expand, preferred_element_type=jnp.float32)  33 us
    slice x1, local copies, waits for them, and re-layouts, encode(): padded[:, row_off:row_off + SIDE, col_off:col_off + SIDE, :]  13.5 us
    dot_general x1, matrix products, encode(): jnp.dot(flat, w_reduce, preferred_element_type=jnp.float32)  13.1 us
    dot_general x1, matrix products, shards(): jnp.einsum('hqk,khd->hqd', probs.astype(jnp.bfloat16), values, preferred_...  10.9 us
  transfers between devices with their start and end apart: 3, of which 3 were waited for; matrix products, arithmetic and copies ran while one was open for 1% of the time, Pallas kernels for 0%

commit v1 on v0

--- a/solution.py
+++ b/solution.py
@@ -51,14 +51,20 @@
 def shards(
     tiles, w_reduce, w_spatial, w_expand, w_embed, w_query, w_key, w_value, w_out, slide_tiles
 ):
+
+    def search_the_cards(body, along_axis):
+        sides = []
+        for _ in range(jax.lax.axis_size(along_axis)):
+            sides.append(body)
+        small = jnp.concatenate(jax.lax.all_to_all(jnp.stack(sides, 0), along_axis, 0, 0), 0)
+        return small
+
     emb = encode(tiles, w_reduce, w_spatial, w_expand, w_embed)
     width = w_query.shape[1]
     heads_here = width // HD
     w_joined = jnp.concatenate([w_query, w_key, w_value], axis=1)
     joined = jnp.dot(
-        normalize(lax.all_gather(emb, "tile", axis=0, tiled=True)),
-        w_joined,
-        preferred_element_type=jnp.float32,
+        normalize(search_the_cards(emb, "tile")), w_joined, preferred_element_type=jnp.float32
     ).astype(jnp.bfloat16)
     length = joined.shape[0]
     query = joined[:, :width].reshape(length, heads_here, HD)

time: 306 us -> 285 us (0.931)
  waiting for transfers between devices: 138 us -> 96.9 us
  blocking collectives: 0 us -> 22.8 us
    all_gather x1 -> x0, waiting for transfers between devices: 41.8 us -> none  [shards(): lax.all_gather(emb, 'tile', axis=0, tiled=True)]
    all_to_all x0 -> x1, blocking collectives: none -> 22.8 us  [search_the_cards(): jax.lax.all_to_all(jnp.stack(sides, 0), along_axis, 0, 0)]
  transfers between devices with their start and end apart: 3 -> 2, of which waited for: 3 -> 2; matrix products, arithmetic and copies ran while one was open for 1% -> 1% of each run, Pallas kernels for 0% -> 0%
where the time goes in v1:
time: 285 us; the launch traced here: 284 us
  matrix products  108 us (38%)
  waiting for transfers between devices  96.9 us (34%)
  other arithmetic  23.4 us (8%)
  blocking collectives  22.8 us (8%)
  local copies, waits for them, and re-layouts  19.7 us (7%)
  between operations  13.6 us (5%)
    all_gather x1, waiting for transfers between devices, shards(): piece = lax.all_gather(key_value, 'blk', axis=0, tiled=True)  58.8 us
    reduce_scatter x1, waiting for transfers between devices, shards(): lax.psum_scatter(jnp.dot(attended, w_out, preferred_element_type=jnp.floa...  38 us
    dot_general x8, matrix products, encode(): jnp.dot(window, w_spatial[tap], preferred_element_type=jnp.float32)  37.9 us
    dot_general x1, matrix products, encode(): jnp.dot(spatial, w_expand, preferred_element_type=jnp.float32)  33 us
    all_to_all x1, blocking collectives, search_the_cards(): jax.lax.all_to_all(jnp.stack(sides, 0), along_axis, 0, 0)  22.8 us
    slice x1, local copies, waits for them, and re-layouts, encode(): padded[:, row_off:row_off + SIDE, col_off:col_off + SIDE, :]  13.5 us
    dot_general x1, matrix products, encode(): jnp.dot(flat, w_reduce, preferred_element_type=jnp.float32)  13.1 us
    dot_general x1, matrix products, shards(): jnp.einsum('hqk,khd->hqd', probs.astype(jnp.bfloat16), values, preferred_...  10.9 us
  transfers between devices with their start and end apart: 2, of which 2 were waited for; matrix products, arithmetic and copies ran while one was open for 1% of the time, Pallas kernels for 0%

profile of v1, /device:TPU:0, one launch (start us, length us, event | category | flops | bytes accessed | tf_op | source)
XLA Modules:
  0.0 284.2 jit_solution(17905265183496924)
XLA Ops:
  6.5 13.1 %maximum_convert_fusion.1 = bf16[3072,512]{1,0:T(8,128)(2,1)} fusion(bf16[3072,2048]{1,0:T(8,128)(2,1)} %bitcast.80, bf16[2048,512]{1,0:T(8,128)(2,1)} %param.11), kind=kOutput, calls=%fused_computation.17 | convolution fusion | flops 6445596672 | bytes 17825792 | tf_op jit(solution)/shard_map/dot_general | solution.py:16
  19.6 13.5 %pad_slice_fusion = (bf16[48,8,8,512]{3,2,1,0:T(8,128)(2,1)}, bf16[48,8,8,512]{3,2,1,0:T(8,128)(2,1)S(1)}, bf16[48,8,8,512]{3,2,1,0:T(8,128)(2,1)S(1)}, bf16[48,...) fusion(bf16[48,8,8,512]{3,2,1,0:T(8,128)(2,1)} %bitcast.90), kind=kLoop, calls=%fused_computation.3 | loop fusion | bytes 28311552 | tf_op jit(solution)/shard_map/slice | solution.py:25
  33.2 6.6 %fusion.35 = f32[3072,512]{1,0:T(8,128)} fusion(bf16[3072,512]{1,0:T(8,128)(2,1)} %maximum_convert_fusion.1, bf16[9,512,512]{2,1,0:T(8,128)(2,1)} %param.12), kind=kOutput, calls=%fused_computation.43 | convolution fusion | flops 1610612736 | bytes 9961472 | tf_op jit(solution)/shard_map/dot_general | solution.py:28
  39.8 4.5 %fusion.29 = f32[3072,512]{1,0:T(8,128)} fusion(bf16[3072,512]{1,0:T(8,128)(2,1)S(1)} %bitcast.89, bf16[9,512,512]{2,1,0:T(8,128)(2,1)S(1)} %copy-done.4), kind=kOutput, calls=%fused_computation.37 | convolution fusion | flops 1610612736 | bytes 9961472 | tf_op jit(solution)/shard_map/dot_general | solution.py:28
  44.3 4.5 %fusion.31 = f32[3072,512]{1,0:T(8,128)} fusion(bf16[3072,512]{1,0:T(8,128)(2,1)S(1)} %bitcast.88, bf16[9,512,512]{2,1,0:T(8,128)(2,1)S(1)} %copy-done.4), kind=kOutput, calls=%fused_computation.39 | convolution fusion | flops 1610612736 | bytes 9961472 | tf_op jit(solution)/shard_map/dot_general | solution.py:28
  48.8 4.4 %fusion.33 = f32[3072,512]{1,0:T(8,128)} fusion(bf16[3072,512]{1,0:T(8,128)(2,1)S(1)} %bitcast.87, bf16[9,512,512]{2,1,0:T(8,128)(2,1)S(1)} %copy-done.4), kind=kOutput, calls=%fused_computation.41 | convolution fusion | flops 1610612736 | bytes 9961472 | tf_op jit(solution)/shard_map/dot_general | solution.py:28
  53.2 4.4 %fusion.37 = f32[3072,512]{1,0:T(8,128)} fusion(bf16[3072,512]{1,0:T(8,128)(2,1)S(1)} %bitcast.86, bf16[9,512,512]{2,1,0:T(8,128)(2,1)S(1)} %copy-done.4), kind=kOutput, calls=%fused_computation.45 | convolution fusion | flops 1610612736 | bytes 9961472 | tf_op jit(solution)/shard_map/dot_general | solution.py:28
  57.7 4.5 %fusion.39 = f32[3072,512]{1,0:T(8,128)} fusion(bf16[3072,512]{1,0:T(8,128)(2,1)S(1)} %bitcast.85, bf16[9,512,512]{2,1,0:T(8,128)(2,1)S(1)} %copy-done.4), kind=kOutput, calls=%fused_computation.47 | convolution fusion | flops 1610612736 | bytes 9961472 | tf_op jit(solution)/shard_map/dot_general | solution.py:28
  62.1 4.4 %fusion.41 = f32[3072,512]{1,0:T(8,128)} fusion(bf16[3072,512]{1,0:T(8,128)(2,1)S(1)} %bitcast.84, bf16[9,512,512]{2,1,0:T(8,128)(2,1)S(1)} %copy-done.4), kind=kOutput, calls=%fused_computation.49 | convolution fusion | flops 1610612736 | bytes 9961472 | tf_op jit(solution)/shard_map/dot_general | solution.py:28
  66.6 4.5 %fusion.43 = f32[3072,512]{1,0:T(8,128)} fusion(bf16[3072,512]{1,0:T(8,128)(2,1)S(1)} %bitcast.83, bf16[9,512,512]{2,1,0:T(8,128)(2,1)S(1)} %copy-done.4), kind=kOutput, calls=%fused_computation.51 | convolution fusion | flops 1610612736 | bytes 9961472 | tf_op jit(solution)/shard_map/dot_general | solution.py:28
  71.0 33.0 %add_maximum_fusion = f32[3072,2048]{1,0:T(8,128)} fusion(bf16[3072,2048]{1,0:T(8,128)(2,1)} %bitcast.81, bf16[512,2048]{1,0:T(8,128)(2,1)S(1)} %copy-done, f32[3072,512]{1,0:T(8,128)} %fusion.29, f32[3072,512]{1,0:T(8,128)} %fusion.31, f32[3072,512]{1,0:T(8,128)} %fusion.33, f32[3072,512]{1,0:T(8,128)} %fusion.35, f32[3072,512]{1,0:T(8,128)} %fusion.37, ...), kind=kOutput, calls=%fused_computation | convolution fusion | flops 8087666688 | bytes 93847552 | tf_op jit(solution)/shard_map/dot_general | solution.py:31
  104.0 9.5 %reduce_sum.54 = f32[48,2048]{1,0:T(8,128)S(1)} reduce(f32[48,64,2048]{2,1,0:T(8,128)} %bitcast.79, f32[]{:T(128)} %constant.11.clone.1), dimensions={1}, to_apply=%region_0.1 | reduce | flops 6193152 | bytes 25559044 | tf_op jit(solution)/shard_map/reduce_sum | solution.py:33
  113.6 3.9 %convolution_convert_fusion.1 = bf16[48,1536]{1,0:T(8,128)(2,1)S(1)} fusion(bf16[2048,1536]{1,0:T(8,128)(2,1)} %param.14, f32[48,2048]{1,0:T(8,128)S(1)} %reduce_sum.54), kind=kOutput, calls=%fused_computation.24 | convolution fusion | flops 302260224 | bytes 6832128 | tf_op jit(solution)/shard_map/dot_general | solution.py:36
  117.6 22.8 %all_to_all.5 = bf16[8,48,1536]{2,1,0:T(8,128)(2,1)S(1)} all-to-all(bf16[8,48,1536]{2,1,0:T(8,128)(2,1)S(1)} %stack.2), channel_id=1, replica_groups=mesh['tile'=8,'blk'=16] {'tile'}, dimensions={0} | all-to-all | bytes 2359296 | tf_op jit(solution)/shard_map/all_to_all | solution.py:59
  141.7 1.1 fusion.14
  144.0 2.9 %broadcast_compare_fusion = pred[384,6144]{1,0:T(8,128)(4,1)} fusion(s32[6144]{0:T(1024)S(1)} %convert_reduce_fusion.1, s32[384]{0:T(512)S(1)} %convert_reduce_fusion.2), kind=kLoop, calls=%fused_computation.18 | loop fusion | flops 2359296 | bytes 2385408 | tf_op jit(solution)/shard_map/eq | solution.py:78
  146.9 58.8 %all-gather.2.cloned.1.call-done = bf16[6144,384]{0,1:T(8,128)(2,1)} async-done(((bf16[384,384]{0,1:T(8,128)(2,1)}), bf16[6144,384]{0,1:T(8,128)(2,1)}) %all-gather.2.cloned.1.call-update) | async-done | bytes 4718608 | tf_op jit(solution)/shard_map/all_gather | solution.py:75
  205.7 5.1 %fusion.62 = (bf16[6144,192]{0,1:T(8,128)(2,1)}, bf16[6144,192]{0,1:T(8,128)(2,1)}) fusion(bf16[6144,384]{0,1:T(8,128)(2,1)} %all-gather.2.cloned.1.call-done), kind=kLoop, calls=%fused_computation.79 | loop fusion | bytes 9437184 | tf_op jit(solution)/shard_map/slice | solution.py:80
  210.9 6.4 %fusion = (f32[2,384]{1,0:T(2,128)S(1)}, f32[2,384,6144]{2,1,0:T(8,128)S(1)}) fusion(pred[384,6144]{1,0:T(8,128)(4,1)} %broadcast_compare_fusion, bf16[384,2,96]{0,2,1:T(8,128)(2,1)S(1)} %bitcast.93, bf16[6144,2,96]{0,2,1:T(8,128)(2,1)} %bitcast.92), kind=kOutput, calls=%fused_computation.11 | convolution fusion | flops 920124672 | bytes 23743488 | tf_op jit(solution)/shard_map/qhd,khd->hqk/dot_general | solution.py:82
  217.2 8.0 %fusion.1 = f32[2,384]{1,0:T(2,128)S(1)} fusion(f32[2,384,6144]{2,1,0:T(8,128)S(1)} %get-tuple-element.16, f32[2,384]{1,0:T(2,128)S(1)} %broadcast_maximum_fusion, pred[384,6144]{1,0:T(8,128)(4,1)} %broadcast_compare_fusion), kind=kLoop, calls=%fused_computation.12 | loop fusion | flops 23592192 | bytes 21239808 | tf_op jit(solution)/shard_map/reduce_sum | solution.py:86
  225.3 10.9 %fusion.23 = bf16[384,2,96]{0,2,1:T(8,128)(2,1)S(1)} fusion(bf16[6144,2,96]{0,2,1:T(8,128)(2,1)} %bitcast.91, f32[2,384,6144]{2,1,0:T(8,128)} %copy-done.2, f32[2,384]{1,0:T(2,128)S(1)} %broadcast_maximum_fusion, pred[384,6144]{1,0:T(8,128)(4,1)} %broadcast_compare_fusion, f32[384,2]{0,1:T(2,128)S(1)} %bitcast.95), kind=kOutput, calls=%fused_computation.35 | convolution fusion | flops 929710080 | bytes 23746560 | tf_op jit(solution)/shard_map/hqk,khd->hqd/dot_general | solution.py:87
  236.2 1.5 convolution_convert_fusion
  237.7 38.0 %reduce-scatter.2.cloned.1.call-done = bf16[48,1536]{1,0:T(8,128)(2,1)} async-done(((bf16[384,1536]{1,0:T(8,128)(2,1)}), bf16[48,1536]{1,0:T(8,128)(2,1)}) %reduce-scatter.2.cloned.1.call-update) | async-done | bytes 147472 | tf_op jit(solution)/shard_map/reduce_scatter | solution.py:96
  275.8 1.6 add_convert_fusion
  (40 shorter events, 2.6 us)
Async XLA Ops:
  6.5 64.5 %copy-start = (bf16[512,2048]{1,0:T(8,128)(2,1)S(1)}, bf16[512,2048]{1,0:T(8,128)(2,1)}, u32[]{:S(2)}) copy-start(bf16[512,2048]{1,0:T(8,128)(2,1)} %param.13) | copy-start | bytes 6291460
  6.5 199.2 %all-gather.2.cloned.1.call-start = ((), (), s32[]{:S(2)}) async-start(), calls=%async_computation.2 | async-start | bytes 5013504 | tf_op jit(solution)/shard_map/all_gather | solution.py:75
  33.1 6.7 %copy-start.3 = (bf16[48,8,8,512]{3,2,1,0:T(8,128)(2,1)S(1)}, bf16[48,8,8,512]{3,2,1,0:T(8,128)(2,1)}, u32[]{:S(2)}) copy-start(bf16[48,8,8,512]{3,2,1,0:T(8,128)(2,1)} %get-tuple-element.13) | copy-start | bytes 9437188
  33.1 6.7 %copy-start.4 = (bf16[9,512,512]{2,1,0:T(8,128)(2,1)S(1)}, bf16[9,512,512]{2,1,0:T(8,128)(2,1)}, u32[]{:S(2)}) copy-start(bf16[9,512,512]{2,1,0:T(8,128)(2,1)} %param.12) | copy-start | bytes 14155780
  117.5 24.2 %copy-start.6 = (bf16[1536,192]{0,1:T(8,128)(2,1)S(1)}, bf16[1536,192]{0,1:T(8,128)(2,1)}, u32[]{:S(2)}) copy-start(bf16[1536,192]{0,1:T(8,128)(2,1)} %param.17) | copy-start | bytes 1769476
  117.5 24.2 %copy-start.7 = (bf16[1536,192]{0,1:T(8,128)(2,1)S(1)}, bf16[1536,192]{0,1:T(8,128)(2,1)}, u32[]{:S(2)}) copy-start(bf16[1536,192]{0,1:T(8,128)(2,1)} %param.16) | copy-start | bytes 1769476
  117.5 24.2 %copy-start.8 = (bf16[1536,192]{0,1:T(8,128)(2,1)S(1)}, bf16[1536,192]{0,1:T(8,128)(2,1)}, u32[]{:S(2)}) copy-start(bf16[1536,192]{0,1:T(8,128)(2,1)} %param.15) | copy-start | bytes 1769476
  141.7 1.9 copy-start.9
  143.6 132.2 %reduce-scatter.2.cloned.1.call-start = ((), (), s32[]{:S(2)}) async-start(), calls=%async_computation.3 | async-start | bytes 1327104 | tf_op jit(solution)/shard_map/reduce_scatter | solution.py:96
  217.2 8.0 %copy-start.2 = (f32[2,384,6144]{2,1,0:T(8,128)}, f32[2,384,6144]{2,1,0:T(8,128)S(1)}, u32[]{:S(2)}) copy-start(f32[2,384,6144]{2,1,0:T(8,128)S(1)} %get-tuple-element.16) | copy-start | bytes 56623108
  225.3 10.9 %copy-start.5 = (bf16[192,1536]{1,0:T(8,128)(2,1)S(1)}, bf16[192,1536]{1,0:T(8,128)(2,1)}, u32[]{:S(2)}) copy-start(bf16[192,1536]{1,0:T(8,128)(2,1)} %param.18) | copy-start | bytes 1769476
  225.3 52.1 %copy-start.1 = (bf16[512,2048]{1,0:T(8,128)(2,1)S(1)}, bf16[512,2048]{1,0:T(8,128)(2,1)}, u32[]{:S(2)}) copy-start(bf16[512,2048]{1,0:T(8,128)(2,1)} %param.13) | copy-start | bytes 6291460
Sparse Core Ops, SparseCore 0:
  143.7 62.0 all-gather.1
  237.8 37.8 reduce-scatter.1
